TPU v7x, 32 devices: a whole 2x2x4 slice. The times are simulated.
32 devices in a mesh: grp: 2 (over x), tile: 8 (over z, y), mem: 2 (over core).
Axes of the slice: x: 2, y: 2, z: 4, core: 2. Of those that a mesh axis runs over, the one named last changes fastest.
Arguments:
- increment: float32 [64, 512, 512], P('grp', 'tile'), parts along dimension 0, may hold values from -6 to 6
- perturbations: bfloat16 [24, 64, 512, 512], P('mem', 'grp', 'tile'), parts along dimension 1, may hold values from -3 to 3
- localization: bfloat16 [18, 256, 256], replicated, may hold values from -1 to 3, as said below
Outputs:
- covariance_product: float32 [64, 512, 512], P('grp', 'tile', 'mem'), parts along dimension 0
There are 2 independent parts, one for each index of `grp`. A program takes and returns all parts, laid end to end along the dimension named above; an argument that names none is the same for every part. Nothing has to cross between parts.
Inputs may be any that keep to these rules, and one draw needn't show every extreme that they name: mode-dependent localization matrices.
All inputs are finite; a program needn't handle non-finite values.
Results may differ from a plain program's by a relative error of at most 0.0052.
Values may be sent and summed in bfloat16 or wider, within the bound.
No kernel may reach another device: no remote copies, remote signals or barrier semaphores. Data moves between devices by JAX's collectives and lax.ppermute only.
A program may use at most 128 MiB of HBM per device.

v0:
```python
import math
import jax
import jax.numpy as jnp
from jax import lax
from jax.sharding import PartitionSpec as P

NX = 512
NY = 512
NZ = 32
MX = 256
MY = 256
MZ = 18


def make_table(modes, cells):
    index = jnp.arange(modes, dtype=jnp.float32)[:, None]
    points = jnp.arange(cells, dtype=jnp.float32)[None, :]
    weights = jnp.where(index == 0, math.sqrt(1.0 / cells), math.sqrt(2.0 / cells))
    return (weights * jnp.cos(math.pi * index * (2.0 * points + 1.0) / (2.0 * cells))).astype(
        jnp.bfloat16
    )


def apply_localization(fields, table_x, localization):
    spectral_weights = jnp.einsum(
        "mync,kn->mcyk", fields, table_x, preferred_element_type=jnp.float32
    ).astype(jnp.bfloat16)
    localized_field = jnp.einsum(
        "aebq,efq->aebf", spectral_weights, localization, preferred_element_type=jnp.float32
    ).astype(jnp.bfloat16)
    return jnp.einsum(
        "mcyl,ln->mync", localized_field, table_x, preferred_element_type=jnp.float32
    ).astype(jnp.bfloat16)


def shards(increment, perturbations, localization):
    members, levels, tile_rows, columns = perturbations.shape
    table_y = make_table(MY, NY)
    table_z = make_table(MZ, NZ)
    table_x = make_table(MX, NX)
    product = (perturbations.astype(jnp.float32) * increment[None]).astype(jnp.bfloat16)
    along_y = jnp.einsum(
        "mzxn,yn->mzxy", product, table_y, preferred_element_type=jnp.float32
    ).astype(jnp.bfloat16)
    along_z = jnp.einsum(
        "cz,mzxy->myxc", table_z, along_y, preferred_element_type=jnp.float32
    ).astype(jnp.bfloat16)
    outgoing = along_z.reshape(members, MY, 1, tile_rows * MZ)
    received = lax.all_to_all(outgoing, "tile", split_axis=1, concat_axis=2, tiled=True)
    member_count = received.shape[0]
    block_list = received.shape[1]
    tile_count = received.shape[2]
    prolonged = apply_localization(
        received.reshape(member_count, block_list, NX, MZ), table_x, localization
    )
    parted = prolonged.reshape(member_count, block_list, tile_count, tile_rows * MZ)
    returned = lax.all_to_all(parted, "tile", split_axis=2, concat_axis=1, tiled=True)
    back = returned.reshape(members, MY, tile_rows, MZ)
    back_z = jnp.einsum("myxc,cz->mzxy", back, table_z, preferred_element_type=jnp.float32).astype(
        jnp.bfloat16
    )
    back_y = jnp.einsum("mzxy,yn->mzxn", back_z, table_y, preferred_element_type=jnp.float32)
    summed = jnp.sum(perturbations.astype(jnp.float32) * back_y, axis=0)
    output_field = lax.psum_scatter(summed, "mem", scatter_dimension=2, tiled=True)
    return output_field


def solution(mesh):
    return jax.shard_map(
        shards,
        mesh=mesh,
        in_specs=(P("grp", "tile", None), P("mem", "grp", "tile", None), P()),
        out_specs=P("grp", "tile", "mem"),
        check_vma=False,
    )
```

profile of v0, /device:TPU:0, one launch (start us, length us, event | category | flops | bytes accessed | tf_op | source)
XLA Modules:
  0.0 950.7 jit_solution(16235727651460496448)
XLA Ops:
  6.5 0.0 copy-start
  6.5 0.0 reduce-scatter.2.cloned.1.call-start
  6.6 24.8 %fusion = bf16[12,32,64,512]{3,2,1,0:T(8,128)(2,1)} fusion(bf16[12,32,64,512]{3,2,1,0:T(8,128)(2,1)} %param.4, f32[32,64,512]{2,1,0:T(8,128)} %param.3), kind=kLoop, calls=%fused_computation.2 | loop fusion | flops 37748736 | bytes 54525952 | tf_op jit(solution)/shard_map/convert_element_type | solution.py:41
  31.4 36.9 %convert_bitcast_fusion.1 = bf16[12,256,64,18]{1,3,2,0:T(8,128)(2,1)} fusion(bf16[12,32,64,512]{3,2,1,0:T(8,128)(2,1)} %fusion, f32[512]{0:T(512)S(1)} %multiply_add_fusion, f32[256]{0:T(256)S(1)} %get-tuple-element.6, f32[256]{0:T(256)S(1)} %get-tuple-element.5, f32[32]{0:T(128)S(1)} %multiply_add_fusion.1, f32[18]{0:T(128)S(1)} %get-tuple-element.8, ...), kind=kOutput, calls=%fused_computation.10 | convolution fusion | flops 6679300096 | bytes 32248080 | tf_op jit(solution)/shard_map/cz,mzxy->myxc/dot_general | solution.py:45
  68.3 12.3 %reshape.53 = bf16[12,256,1,1152]{1,3,0,2:T(8,128)(2,1)} reshape(bf16[12,256,64,18]{1,3,2,0:T(8,128)(2,1)} %convert_bitcast_fusion.1) | data formatting | bytes 14155776 | tf_op jit(solution)/shard_map/reshape | solution.py:48
  80.7 12.5 %copy.9 = bf16[12,256,1,1152]{3,0,2,1:T(8,128)(2,1)} copy(bf16[12,256,1,1152]{1,3,0,2:T(8,128)(2,1)} %reshape.53) | data formatting | bytes 14155776 | tf_op jit(solution)/shard_map/reshape | solution.py:48
  93.2 226.1 %all_to_all.30 = bf16[12,256,1,1152]{3,0,2,1:T(8,128)(2,1)} all-to-all(bf16[12,256,1,1152]{3,0,2,1:T(8,128)(2,1)} %copy.9), channel_id=1, replica_groups=mesh['grp'=2,'tile'=8,'mem'=2] {'tile'}, dimensions={1} | all-to-all | bytes 14155776 | tf_op jit(solution)/shard_map/all_to_all | solution.py:49
  319.3 5.3 copy.10
  324.7 5.7 copy.11
  330.3 123.3 %reshape.54 = bf16[12,32,512,18]{3,2,1,0:T(8,128)(2,1)} reshape(bf16[12,32,8,1,1152]{4,2,1,0,3:T(8,128)(2,1)} %copy.11) | data formatting | bytes 14155776 | tf_op jit(solution)/shard_map/reshape | solution.py:54
  453.6 43.7 %copy.12 = bf16[12,32,512,18]{2,1,3,0:T(8,128)(2,1)} copy(bf16[12,32,512,18]{3,2,1,0:T(8,128)(2,1)} %reshape.54) | data formatting | bytes 14155776 | tf_op jit(solution)/shard_map/reshape | solution.py:54
  497.3 10.2 %fusion.29 = bf16[256,12,32,18]{0,2,3,1:T(8,128)(2,1)} fusion(bf16[12,32,512,18]{2,1,3,0:T(8,128)(2,1)} %copy.12, f32[512]{0:T(512)S(1)} %multiply_add_fusion, f32[256]{0:T(256)S(1)} %get-tuple-element.6, f32[256]{0:T(256)S(1)} %get-tuple-element.5), kind=kOutput, calls=%fused_computation.20 | convolution fusion | flops 1812463616 | bytes 10620928 | tf_op jit(solution)/shard_map/mync,kn->mcyk/dot_general | solution.py:25
  507.5 0.0 copy-done
  507.5 9.5 convert_bitcast_fusion.2
  517.0 41.2 %copy.13 = bf16[12,32,512,18]{3,2,1,0:T(8,128)(2,1)} copy(bf16[12,32,512,18]{2,1,3,0:T(8,128)(2,1)} %convert_bitcast_fusion.2) | data formatting | bytes 14155776 | tf_op jit(solution)/shard_map/convert_element_type | solution.py:33
  558.2 71.0 %reshape.55 = bf16[12,32,8,1152]{3,2,1,0:T(8,128)(2,1)} reshape(bf16[12,32,512,18]{3,2,1,0:T(8,128)(2,1)} %copy.13) | data formatting | bytes 14155776 | tf_op jit(solution)/shard_map/reshape | solution.py:56
  629.2 4.0 copy.14
  633.3 158.3 %all_to_all.31 = bf16[12,32,8,1152]{3,1,0,2:T(8,128)(2,1)} all-to-all(bf16[12,32,8,1152]{3,1,0,2:T(8,128)(2,1)S(1)} %copy.14), channel_id=1, replica_groups=mesh['grp'=2,'tile'=8,'mem'=2] {'tile'}, dimensions={2} | all-to-all | bytes 14155776 | tf_op jit(solution)/shard_map/all_to_all | solution.py:57
  791.6 25.2 %copy.15 = bf16[12,8,32,1,1152]{2,1,4,0,3:T(8,128)(2,1)} copy(bf16[12,8,32,1,1152]{4,2,0,1,3:T(8,128)(2,1)} %bitcast.56) | data formatting | bytes 14155776 | tf_op jit(solution)/shard_map/all_to_all | solution.py:57
  816.8 36.4 %reshape.56 = bf16[12,256,64,18]{1,3,2,0:T(8,128)(2,1)} reshape(bf16[12,8,32,1,1152]{2,1,4,0,3:T(8,128)(2,1)} %copy.15) | data formatting | bytes 14155776 | tf_op jit(solution)/shard_map/reshape | solution.py:58
  853.1 9.0 convert_bitcast_fusion
  862.1 0.0 copy-start.1
  862.1 70.3 %fusion.1 = f32[32,64,512]{2,1,0:T(8,128)} fusion(bf16[12,32,64,512]{3,2,1,0:T(8,128)(2,1)} %param.4, bf16[12,32,64,256]{3,1,2,0:T(8,128)(2,1)} %convert_bitcast_fusion, f32[512]{0:T(512)S(1)} %multiply_add_fusion, f32[256]{0:T(256)S(1)} %get-tuple-element.6, f32[256]{0:T(256)S(1)} %get-tuple-element.5), kind=kOutput, calls=%fused_computation.3 | convolution fusion | flops 6479675392 | bytes 41947136 | tf_op jit(solution)/shard_map/mzxy,yn->mzxn/dot_general | solution.py:62
  932.5 0.0 reduce-scatter.2.cloned.1.call-update
  932.5 10.9 %reduce-scatter.2.cloned.1.call-done = f32[32,64,256]{2,1,0:T(8,128)} async-done(((f32[32,64,512]{2,1,0:T(8,128)}), f32[32,64,256]{2,1,0:T(8,128)}) %reduce-scatter.2.cloned.1.call-update) | async-done | bytes 2097168 | tf_op jit(solution)/shard_map/reduce_scatter | solution.py:64
  943.4 0.0 copy-done.1
  (4 shorter events, 0.0 us)
Async XLA Ops:
  6.5 501.0 %copy-start = (bf16[18,256,256]{2,1,0:T(8,128)(2,1)S(1)}, bf16[18,256,256]{2,1,0:T(8,128)(2,1)}, u32[]{:S(2)}) copy-start(bf16[18,256,256]{2,1,0:T(8,128)(2,1)} %param.5) | copy-start | bytes 7077892
  6.5 936.9 %reduce-scatter.2.cloned.1.call-start = ((), (), s32[]{:S(2)}) async-start(), calls=%async_computation.3 | async-start | bytes 6291456 | tf_op jit(solution)/shard_map/reduce_scatter | solution.py:64
  862.1 81.3 %copy-start.1 = (bf16[18,256,256]{2,1,0:T(8,128)(2,1)S(1)}, bf16[18,256,256]{2,1,0:T(8,128)(2,1)}, u32[]{:S(2)}) copy-start(bf16[18,256,256]{2,1,0:T(8,128)(2,1)} %param.5) | copy-start | bytes 7077892
Sparse Core Ops, SparseCore 0:
  932.6 10.7 reduce-scatter.1
where the time goes:
time: 964 us; the launch traced here: 951 us
  blocking collectives  384 us (40%)
  local copies, waits for them, and re-layouts  381 us (40%)
  matrix products  136 us (14%)
  other arithmetic  24.9 us (3%)
  between operations  13.8 us (1%)
  waiting for transfers between devices  11 us (1%)
    all_to_all x1, blocking collectives, shards(): lax.all_to_all(outgoing, 'tile', split_axis=1, concat_axis=2, tiled=True)  226 us
    reshape x2, local copies, waits for them, and re-layouts, shards(): received.reshape(member_count, block_list, NX, MZ)  167 us
    all_to_all x1, blocking collectives, shards(): lax.all_to_all(parted, 'tile', split_axis=2, concat_axis=1, tiled=True)  158 us
    reshape x2, local copies, waits for them, and re-layouts, shards(): prolonged.reshape(member_count, block_list, tile_count, tile_rows * MZ)  75 us
    dot_general x1, matrix products, shards(): jnp.einsum('mzxy,yn->mzxn', back_z, table_y, preferred_element_type=jnp.f...  70.3 us
    convert_element_type x1, local copies, waits for them, and re-layouts, apply_localization(): return jnp.einsum('mcyl,ln->mync', localized_field, table_x, preferred_el...  41.2 us
    dot_general x1, matrix products, shards(): jnp.einsum('cz,mzxy->myxc', table_z, along_y, preferred_element_type=jnp....  36.9 us
    reshape x1, local copies, waits for them, and re-layouts, shards(): back = returned.reshape(members, MY, tile_rows, MZ)  36.4 us
  transfers between devices with their start and end apart: 1, of which 1 were waited for; matrix products, arithmetic and copies ran while one was open for 0% of the time, Pallas kernels for 0%

commit v1 on v0

--- a/solution.py
+++ b/solution.py
@@ -54,7 +54,10 @@
         received.reshape(member_count, block_list, NX, MZ), table_x, localization
     )
     parted = prolonged.reshape(member_count, block_list, tile_count, tile_rows * MZ)
-    returned = lax.all_to_all(parted, "tile", split_axis=2, concat_axis=1, tiled=True)
+    returned = jnp.concatenate(
+        lax.all_to_all(jnp.stack(jnp.split(parted, lax.axis_size("tile"), axis=2)), "tile", 0, 0),
+        axis=1,
+    )
     back = returned.reshape(members, MY, tile_rows, MZ)
     back_z = jnp.einsum("myxc,cz->mzxy", back, table_z, preferred_element_type=jnp.float32).astype(
         jnp.bfloat16

time: 964 us -> 982 us (1.019)
  local copies, waits for them, and re-layouts: 381 us -> 412 us
  blocking collectives: 384 us -> 372 us
    another operation x0 -> x2, local copies, waits for them, and re-layouts: none -> 36.6 us  [the longest x1 36.4 us: shards(): back = returned.reshape(members, MY, tile_rows, MZ)]
    split x0 -> x1, local copies, waits for them, and re-layouts: none -> 33.8 us  [shards(): jnp.split(parted, lax.axis_size('tile'), axis=2)]
    all_to_all x1 -> x0, local copies, waits for them, and re-layouts: 25.2 us -> none  [shards(): lax.all_to_all(parted, 'tile', split_axis=2, concat_axis=1, tiled=True)]
    all_to_all x1, blocking collectives: 226 us -> 213 us  [shards(): lax.all_to_all(outgoing, 'tile', split_axis=1, concat_axis=2, tiled=True)]
    reshape x1, local copies, waits for them, and re-layouts: 36.4 us -> 25.2 us  [shards(): jnp.concatenate(lax.all_to_all(jnp.stack(jnp.split(parted, lax.axis_size(...]
    reshape x2 -> x1, local copies, waits for them, and re-layouts: 75 us -> 71 us  [shards(): prolonged.reshape(member_count, block_list, tile_count, tile_rows * MZ)]
where the time goes in v1:
time: 982 us; the launch traced here: 969 us
  local copies, waits for them, and re-layouts  412 us (42%)
  blocking collectives  372 us (38%)
  matrix products  136 us (14%)
  other arithmetic  24.8 us (3%)
  between operations  13.7 us (1%)
  waiting for transfers between devices  10.9 us (1%)
    all_to_all x1, blocking collectives, shards(): lax.all_to_all(outgoing, 'tile', split_axis=1, concat_axis=2, tiled=True)  213 us
    reshape x2, local copies, waits for them, and re-layouts, shards(): received.reshape(member_count, block_list, NX, MZ)  167 us
    all_to_all x1, blocking collectives, shards(): lax.all_to_all(jnp.stack(jnp.split(parted, lax.axis_size('tile'), axis=2)...  158 us
    reshape x1, local copies, waits for them, and re-layouts, shards(): prolonged.reshape(member_count, block_list, tile_count, tile_rows * MZ)  71 us
    dot_general x1, matrix products, shards(): jnp.einsum('mzxy,yn->mzxn', back_z, table_y, preferred_element_type=jnp.f...  70.3 us
    convert_element_type x1, local copies, waits for them, and re-layouts, apply_localization(): return jnp.einsum('mcyl,ln->mync', localized_field, table_x, preferred_el...  41.6 us
    dot_general x1, matrix products, shards(): jnp.einsum('cz,mzxy->myxc', table_z, along_y, preferred_element_type=jnp....  36.9 us
    another operation x1, local copies, waits for them, and re-layouts, shards(): back = returned.reshape(members, MY, tile_rows, MZ)  36.4 us
  transfers between devices with their start and end apart: 1, of which 1 were waited for; matrix products, arithmetic and copies ran while one was open for 0% of the time, Pallas kernels for 0%

profile of v1, /device:TPU:0, one launch (start us, length us, event | category | flops | bytes accessed | tf_op | source)
XLA Modules:
  0.0 969.5 jit_solution(15393597450581960094)
XLA Ops:
  6.5 0.0 copy-start
  6.5 0.0 reduce-scatter.2.cloned.1.call-start
  6.6 24.8 %fusion = bf16[12,32,64,512]{3,2,1,0:T(8,128)(2,1)} fusion(bf16[12,32,64,512]{3,2,1,0:T(8,128)(2,1)} %param.4, f32[32,64,512]{2,1,0:T(8,128)} %param.3), kind=kLoop, calls=%fused_computation.2 | loop fusion | flops 37748736 | bytes 54525952 | tf_op jit(solution)/shard_map/convert_element_type | solution.py:41
  31.4 36.9 %convert_bitcast_fusion.1 = bf16[12,256,64,18]{1,3,2,0:T(8,128)(2,1)} fusion(bf16[12,32,64,512]{3,2,1,0:T(8,128)(2,1)} %fusion, f32[512]{0:T(512)S(1)} %multiply_add_fusion, f32[256]{0:T(256)S(1)} %get-tuple-element.14, f32[256]{0:T(256)S(1)} %get-tuple-element.13, f32[32]{0:T(128)S(1)} %multiply_add_fusion.1, f32[18]{0:T(128)S(1)} %get-tuple-element.16, ...), kind=kOutput, calls=%fused_computation.10 | convolution fusion | flops 6679300096 | bytes 32248080 | tf_op jit(solution)/shard_map/cz,mzxy->myxc/dot_general | solution.py:45
  68.3 12.3 %reshape.52 = bf16[12,256,1,1152]{1,3,0,2:T(8,128)(2,1)} reshape(bf16[12,256,64,18]{1,3,2,0:T(8,128)(2,1)} %convert_bitcast_fusion.1) | data formatting | bytes 14155776 | tf_op jit(solution)/shard_map/reshape | solution.py:48
  80.7 12.5 %copy.86 = bf16[12,256,1,1152]{3,0,2,1:T(8,128)(2,1)} copy(bf16[12,256,1,1152]{1,3,0,2:T(8,128)(2,1)} %reshape.52) | data formatting | bytes 14155776 | tf_op jit(solution)/shard_map/reshape | solution.py:48
  93.2 213.4 %all_to_all.20 = bf16[12,256,1,1152]{3,0,2,1:T(8,128)(2,1)} all-to-all(bf16[12,256,1,1152]{3,0,2,1:T(8,128)(2,1)} %copy.86), channel_id=1, replica_groups=mesh['grp'=2,'tile'=8,'mem'=2] {'tile'}, dimensions={1} | all-to-all | bytes 14155776 | tf_op jit(solution)/shard_map/all_to_all | solution.py:49
  306.6 5.3 copy.87
  311.9 5.7 copy.88
  317.6 123.3 %reshape.53 = bf16[12,32,512,18]{3,2,1,0:T(8,128)(2,1)} reshape(bf16[12,32,8,1,1152]{4,2,1,0,3:T(8,128)(2,1)} %copy.88) | data formatting | bytes 14155776 | tf_op jit(solution)/shard_map/reshape | solution.py:54
  440.8 43.7 %copy.89 = bf16[12,32,512,18]{2,1,3,0:T(8,128)(2,1)} copy(bf16[12,32,512,18]{3,2,1,0:T(8,128)(2,1)} %reshape.53) | data formatting | bytes 14155776 | tf_op jit(solution)/shard_map/reshape | solution.py:54
  484.6 10.2 %fusion.29 = bf16[256,12,32,18]{0,2,3,1:T(8,128)(2,1)} fusion(bf16[12,32,512,18]{2,1,3,0:T(8,128)(2,1)} %copy.89, f32[512]{0:T(512)S(1)} %multiply_add_fusion, f32[256]{0:T(256)S(1)} %get-tuple-element.14, f32[256]{0:T(256)S(1)} %get-tuple-element.13), kind=kOutput, calls=%fused_computation.28 | convolution fusion | flops 1812463616 | bytes 10620928 | tf_op jit(solution)/shard_map/mync,kn->mcyk/dot_general | solution.py:25
  494.7 0.0 copy-done
  494.7 9.5 convert_bitcast_fusion.2
  504.2 41.6 %copy.90 = bf16[12,32,512,18]{3,2,1,0:T(8,128)(2,1)} copy(bf16[12,32,512,18]{2,1,3,0:T(8,128)(2,1)} %convert_bitcast_fusion.2) | data formatting | bytes 14155776 | tf_op jit(solution)/shard_map/convert_element_type | solution.py:33
  545.8 71.0 %reshape.54 = bf16[12,32,8,1152]{3,2,1,0:T(8,128)(2,1)} reshape(bf16[12,32,512,18]{3,2,1,0:T(8,128)(2,1)} %copy.90) | data formatting | bytes 14155776 | tf_op jit(solution)/shard_map/reshape | solution.py:56
  616.9 33.8 %fusion.64 = (bf16[12,32,1,1152]{3,2,1,0:T(2,128)(2,1)S(1)}, bf16[12,32,1,1152]{3,2,1,0:T(2,128)(2,1)S(1)}, bf16[12,32,1,1152]{3,2,1,0:T(2,128)(2,1)S(1)}, bf16[...) fusion(bf16[12,32,8,1152]{3,2,1,0:T(8,128)(2,1)} %reshape.54), kind=kLoop, calls=%fused_computation.61 | loop fusion | bytes 14155776 | tf_op jit(solution)/shard_map/split | solution.py:58
  650.7 0.1 bitcast_dynamic-update-slice_fusion.7
  650.9 0.2 bitcast_dynamic-update-slice_fusion.6
  651.1 0.2 bitcast_dynamic-update-slice_fusion.5
  651.3 0.2 bitcast_dynamic-update-slice_fusion.4
  651.4 0.2 bitcast_dynamic-update-slice_fusion.3
  651.6 0.2 bitcast_dynamic-update-slice_fusion.2
  651.8 0.2 bitcast_dynamic-update-slice_fusion.1
  652.0 0.2 bitcast_dynamic-update-slice_fusion
  652.2 158.4 %all_to_all.21 = bf16[8,12,32,1,1152]{4,2,1,3,0:T(8,128)(2,1)} all-to-all(bf16[8,12,32,1,1152]{4,2,1,3,0:T(8,128)(2,1)S(1)} %bitcast_dynamic-update-slice_fusion), channel_id=1, replica_groups=mesh['grp'=2,'tile'=8,'mem'=2] {'tile'}, dimensions={0} | all-to-all | bytes 14155776 | tf_op jit(solution)/shard_map/all_to_all | solution.py:58
  810.6 25.2 %copy.91 = bf16[12,8,32,1,1152]{2,1,4,0,3:T(8,128)(2,1)} copy(bf16[12,8,32,1,1152]{4,2,0,3,1:T(8,128)(2,1)} %bitcast.70) | data formatting | bytes 14155776 | tf_op jit(solution)/shard_map/reshape | solution.py:57
  835.8 36.4 %reshape_reshape.3 = bf16[12,256,64,18]{1,3,2,0:T(8,128)(2,1)} reshape(bf16[12,8,32,1,1152]{2,1,4,0,3:T(8,128)(2,1)} %copy.91) | data formatting | bytes 14155776 | tf_op jit(solution)/shard_map/reshape;reshape | solution.py:61
  872.2 9.0 convert_bitcast_fusion
  881.2 70.3 %fusion.1 = f32[32,64,512]{2,1,0:T(8,128)} fusion(bf16[12,32,64,512]{3,2,1,0:T(8,128)(2,1)} %param.4, bf16[12,32,64,256]{3,1,2,0:T(8,128)(2,1)} %convert_bitcast_fusion, f32[512]{0:T(512)S(1)} %multiply_add_fusion, f32[256]{0:T(256)S(1)} %get-tuple-element.14, f32[256]{0:T(256)S(1)} %get-tuple-element.13), kind=kOutput, calls=%fused_computation.3 | convolution fusion | flops 6479675392 | bytes 41947136 | tf_op jit(solution)/shard_map/mzxy,yn->mzxn/dot_general | solution.py:65
  951.5 0.0 reduce-scatter.2.cloned.1.call-update
  951.5 10.9 %reduce-scatter.2.cloned.1.call-done = f32[32,64,256]{2,1,0:T(8,128)} async-done(((f32[32,64,512]{2,1,0:T(8,128)}), f32[32,64,256]{2,1,0:T(8,128)}) %reduce-scatter.2.cloned.1.call-update) | async-done | bytes 2097168 | tf_op jit(solution)/shard_map/reduce_scatter | solution.py:67
  (6 shorter events, 0.0 us)
Async XLA Ops:
  6.5 488.2 %copy-start = (bf16[18,256,256]{2,1,0:T(8,128)(2,1)S(1)}, bf16[18,256,256]{2,1,0:T(8,128)(2,1)}, u32[]{:S(2)}) copy-start(bf16[18,256,256]{2,1,0:T(8,128)(2,1)} %param.5) | copy-start | bytes 7077892
  6.5 955.9 %reduce-scatter.2.cloned.1.call-start = ((), (), s32[]{:S(2)}) async-start(), calls=%async_computation.3 | async-start | bytes 6291456 | tf_op jit(solution)/shard_map/reduce_scatter | solution.py:67
  881.1 81.3 %copy-start.1 = (bf16[18,256,256]{2,1,0:T(8,128)(2,1)S(1)}, bf16[18,256,256]{2,1,0:T(8,128)(2,1)}, u32[]{:S(2)}) copy-start(bf16[18,256,256]{2,1,0:T(8,128)(2,1)} %param.5) | copy-start | bytes 7077892
Sparse Core Ops, SparseCore 0:
  951.6 10.7 reduce-scatter.1
